TPU v7x, 32 devices: a whole 2x2x4 slice. The times are simulated.
32 devices in a mesh: ab: 2 (over y), cd: 16 (over z, x, core).
Axes of the slice: x: 2, y: 2, z: 4, core: 2. Of those that a mesh axis runs over, the one named last changes fastest.
Arguments:
- amplitudes: float32 [768, 16384], P('cd', 'ab'), may hold values from -1.25 to 1.25
- driver: float32 [768, 16384], P('cd', 'ab'), may hold values from -6 to 6
- ladder: bfloat16 [16384, 16384], P('ab', 'cd'), may hold values from -0.125 to 0.125
- block_mask: int32 [128, 128], P('ab', 'cd'), may hold values 0 or 1
- pair_list: int32 [768], replicated, may hold values from 0 to 1023, as said below
- occ_energy: float32 [32], replicated, may hold values from -2 to -0.5
- virt_energy: float32 [128], replicated, may hold values from 0.5 to 3
Outputs:
- new_amplitudes: float32 [768, 16384], P('cd', 'ab')
Inputs may be any that keep to these rules, and one draw needn't show every extreme that they name: `pair_list`: the entries are distinct occupied pairs i * 32 + j. Rows come in aligned blocks of two: a pair with i != j shares its block with the pair (j, i); pairs with i == j stand two to a block. Pairs 0 and 1023 are always listed.
All inputs are finite; a program needn't handle non-finite values. No bound on the sum of `block_mask` on one device may be relied on, other than what follows from the above.
Results may differ from a plain program's by a relative error of at most 0.008.
Values may be sent and summed in bfloat16 or wider, within the bound.
A program may use at most 128 MiB of HBM per device.

v0:
```python
import jax
import jax.numpy as jnp
from jax import lax
from jax.sharding import PartitionSpec as P

NV = 128
NOCC = 32
BLK = 128
ITERS = 2


def flip_tiles(tiles, tile_width):
    row_count, tile_count = tiles.shape[:2]
    turned = jnp.swapaxes(tiles.reshape(row_count, tile_count, tile_width, tile_width), 2, 3)
    return turned.reshape(row_count, tile_count * tile_width * tile_width)


def body(amplitudes, driver, ladder, block_mask, pair_list, occ_energy, virt_energy):
    ab_count = lax.axis_size("ab")
    ab_index = lax.axis_index("ab")
    cd_index = lax.axis_index("cd")
    rows_dev, cols_dev = amplitudes.shape
    out_rows, in_cols = ladder.shape
    tile_width = NV // ab_count
    tile_area = tile_width * tile_width
    weights = ladder.reshape(out_rows // BLK, BLK, in_cols // BLK, BLK)
    weights = (weights * block_mask.astype(jnp.bfloat16)[:, None, :, None]).reshape(
        out_rows, in_cols
    )
    pairs_local = ab_index * cols_dev + jnp.arange(cols_dev, dtype=jnp.int32)
    big_a = pairs_local // (tile_width * NV)
    big_b = pairs_local // tile_area % ab_count
    first = big_a * tile_width + pairs_local // tile_width % tile_width
    second = big_b * tile_width + pairs_local % tile_width
    virt_index = jnp.arange(NV, dtype=jnp.int32)
    picks = (first[:, None] == virt_index).astype(jnp.float32) + (
        second[:, None] == virt_index
    ).astype(jnp.float32)
    col_energy = jnp.dot(picks, virt_energy, precision=lax.Precision.HIGHEST)
    row_pairs = lax.dynamic_slice_in_dim(pair_list, cd_index * rows_dev, rows_dev)
    occ_index = jnp.arange(NOCC, dtype=jnp.int32)
    occ_picks = (row_pairs[:, None] // NOCC == occ_index).astype(jnp.float32)
    occ_picks = occ_picks + (row_pairs[:, None] % NOCC == occ_index).astype(jnp.float32)
    row_energy = jnp.dot(occ_picks, occ_energy, precision=lax.Precision.HIGHEST)
    denominator = col_energy[None, :] - row_energy[:, None]
    local_diagonal = row_pairs // NOCC == row_pairs % NOCC
    row_index = jnp.arange(rows_dev, dtype=jnp.int32)
    mirror_row = jnp.where(local_diagonal, row_index, row_index ^ 1)
    row_swap = (mirror_row[:, None] == row_index).astype(jnp.bfloat16)
    state = amplitudes
    for step in range(ITERS):
        rounded = state.astype(jnp.bfloat16)
        regrouped = lax.all_to_all(rounded, "cd", split_axis=1, concat_axis=0, tiled=True)
        partial_value = lax.dot_general(
            lax.all_gather(regrouped, "ab", axis=1, tiled=True),
            weights,
            (((1,), (1,)), ((), ())),
            preferred_element_type=jnp.float32,
        )
        received = lax.psum_scatter(
            partial_value.astype(jnp.bfloat16), "cd", scatter_dimension=0, tiled=True
        )
        swapped = jnp.dot(row_swap, received, preferred_element_type=jnp.float32)
        tiles = lax.all_to_all(
            swapped.astype(jnp.bfloat16).reshape(rows_dev, ab_count, tile_area),
            "ab",
            split_axis=1,
            concat_axis=1,
            tiled=True,
        )
        symmetric = received.astype(jnp.float32) + flip_tiles(tiles, tile_width).astype(jnp.float32)
        state = (driver + symmetric) / denominator
    return state


def solution(mesh):
    placed = (P("cd", "ab"), P("cd", "ab"), P("ab", "cd"), P("ab", "cd"), P(), P(), P())
    return jax.shard_map(body, mesh=mesh, in_specs=placed, out_specs=P("cd", "ab"), check_vma=False)
```

profile of v0, /device:TPU:0, one launch (start us, length us, event | category | flops | bytes accessed | tf_op | source)
XLA Modules:
  0.0 506.5 jit_solution(11198391696417357768)
XLA Ops:
  8.1 27.4 %all_to_all.48 = bf16[48,16,512]{2,0,1:T(8,128)(2,1)} all-to-all(bf16[48,16,512]{2,0,1:T(8,128)(2,1)S(1)} %bitcast.62), channel_id=1, replica_groups=mesh['ab'=2,'cd'=16] {'cd'}, dimensions={1} | all-to-all | bytes 1572864 | tf_op jit(solution)/shard_map/all_to_all | solution.py:53
  35.7 26.5 %all-gather.3.cloned.1.call-done = bf16[768,1024]{1,0:T(8,128)(2,1)} async-done(((bf16[768,512]{1,0:T(8,128)(2,1)}), bf16[768,1024]{1,0:T(8,128)(2,1)}) %all-gather.3.cloned.1.call-update) | async-done | bytes 1572880 | tf_op jit(solution)/shard_map/all_gather | solution.py:55
  62.2 6.1 %mul.31 = bf16[64,128,8,128]{3,2,1,0:T(8,128)(2,1)} broadcast(bf16[64,8]{1,0:T(8,128)(2,1)S(1)} %copy.52), dimensions={0,2} | broadcast | bytes 16778240 | tf_op jit(solution)/shard_map/mul | solution.py:27
  68.3 22.4 %fusion = bf16[768,8192]{0,1:T(8,128)(2,1)} fusion(bf16[768,1024]{1,0:T(8,128)(2,1)S(1)} %copy-done.3, bf16[8192,1024]{1,0:T(8,128)(2,1)} %param.9, bf16[1024,8,8,128]{3,2,1,0:T(8,128)(2,1)} %bitcast.55), kind=kOutput, calls=%fused_computation.3 | convolution fusion | flops 12899581952 | bytes 47710208 | tf_op jit(solution)/shard_map/dot_general | solution.py:54
  90.7 16.7 %copy.62 = bf16[768,8192]{1,0:T(8,128)(2,1)} copy(bf16[768,8192]{0,1:T(8,128)(2,1)} %fusion) | data formatting | bytes 25165824
  108.2 134.3 %reduce-scatter.7.cloned.1.call-done = bf16[48,8192]{1,0:T(8,128)(2,1)} async-done(((bf16[768,8192]{1,0:T(8,128)(2,1)}), bf16[48,8192]{1,0:T(8,128)(2,1)}) %reduce-scatter.7.cloned.1.call-update) | async-done | bytes 786448
  242.5 1.5 convolution_convert_fusion.3
  244.9 3.5 all-to-all-start.1
  248.8 6.4 %fusion.1 = f32[1,8192]{1,0:T(1,128)S(1)} fusion(s32[8192]{0:T(1024)S(1)} %get-tuple-element.9, s32[8192]{0:T(1024)S(1)} %get-tuple-element.8, f32[128]{0:T(128)S(1)} %copy-done), kind=kOutput, calls=%fused_computation.6 | convolution fusion | flops 17825792 | bytes 98816 | tf_op jit(solution)/shard_map/dot_general | solution.py:39
  255.3 3.5 all-to-all-done.1
  258.7 2.4 reshape.139
  261.1 2.4 copy.56
  263.5 1.9 reshape.137
  265.4 2.5 fusion.7
  268.0 25.0 %all_to_all.49 = bf16[48,16,512]{2,0,1:T(8,128)(2,1)} all-to-all(bf16[48,16,512]{2,0,1:T(8,128)(2,1)S(1)} %bitcast.63), channel_id=1, replica_groups=mesh['ab'=2,'cd'=16] {'cd'}, dimensions={1} | all-to-all | bytes 1572864 | tf_op jit(solution)/shard_map/all_to_all | solution.py:53
  293.2 25.5 %all-gather.5.cloned.1.call-done = bf16[768,1024]{1,0:T(8,128)(2,1)} async-done(((bf16[768,512]{1,0:T(8,128)(2,1)}), bf16[768,1024]{1,0:T(8,128)(2,1)}) %all-gather.5.cloned.1.call-update) | async-done | bytes 1572880 | tf_op jit(solution)/shard_map/all_gather | solution.py:55
  318.7 21.7 %convolution_convert_fusion = bf16[768,8192]{1,0:T(8,128)(2,1)} fusion(bf16[768,1024]{1,0:T(8,128)(2,1)} %all-gather.5.cloned.1.call-done, bf16[8192,1024]{1,0:T(8,128)(2,1)} %param.9, bf16[1024,8,8,128]{3,2,1,0:T(8,128)(2,1)} %bitcast.56), kind=kOutput, calls=%fused_computation.1 | convolution fusion | flops 12899581952 | bytes 47710208 | tf_op jit(solution)/shard_map/dot_general | solution.py:54
  340.4 135.0 %reduce-scatter.9.cloned.1.call-done = bf16[48,8192]{1,0:T(8,128)(2,1)} async-done(((bf16[768,8192]{1,0:T(8,128)(2,1)}), bf16[48,8192]{1,0:T(8,128)(2,1)}) %reduce-scatter.9.cloned.1.call-update) | async-done | bytes 786448
  475.4 1.5 convolution_convert_fusion.2
  477.0 12.7 %all_to_all.50 = bf16[48,2,4096]{2,0,1:T(8,128)(2,1)S(1)} all-to-all(bf16[48,2,4096]{2,0,1:T(8,128)(2,1)S(1)} %bitcast.65), channel_id=1, replica_groups=mesh['ab'=2,'cd'=16] {'ab'}, dimensions={1} | all-to-all | bytes 1572864 | tf_op jit(solution)/shard_map/all_to_all | solution.py:64
  489.7 2.4 reshape.140
  492.1 2.4 copy.61
  494.5 1.9 reshape.138
  496.4 3.6 subtract_divide_fusion
  (28 shorter events, 4.2 us)
Async XLA Ops:
  6.5 242.3 %copy-start = (f32[128]{0:T(128)S(1)}, f32[128]{0:T(128)}, u32[]{:S(2)}) copy-start(f32[128]{0:T(128)} %param.13) | copy-start | bytes 1540
  6.5 29.1 %copy-start.2 = (s32[64,8]{0,1:T(8,128)S(1)}, s32[64,8]{0,1:T(8,128)}, u32[]{:S(2)}) copy-start(s32[64,8]{0,1:T(8,128)} %param.10) | copy-start | bytes 6148
  6.5 55.7 %all-gather.3.cloned.1.call-start = ((), (), s32[]{:S(2)}) async-start(), calls=%async_computation.6 | async-start | bytes 2359296 | tf_op jit(solution)/shard_map/all_gather | solution.py:55
  35.6 206.9 %reduce-scatter.7.cloned.1.call-start = ((), (), s32[]{:S(2)}) async-start(), calls=%async_computation.8 | async-start | bytes 13369344
  62.2 6.1 %copy-start.3 = (bf16[768,1024]{1,0:T(8,128)(2,1)S(1)}, bf16[768,1024]{1,0:T(8,128)(2,1)}, u32[]{:S(2)}) copy-start(bf16[768,1024]{1,0:T(8,128)(2,1)} %all-gather.3.cloned.1.call-done) | copy-start | bytes 4718596
  107.4 141.2 %copy-start.4 = (f32[32]{0:T(128)S(1)}, f32[32]{0:T(128)}, u32[]{:S(2)}) copy-start(f32[32]{0:T(128)} %param.12) | copy-start | bytes 388
  244.9 13.8 %all-to-all-start.1 = ((bf16[48,2,4096]{2,0,1:T(8,128)(2,1)}), bf16[48,2,4096]{2,0,1:T(8,128)(2,1)S(1)}, u32[]{:S(2)}, u32[]{:S(2)}) async-start(bf16[48,2,4096]{2,0,1:T(8,128)(2,1)} %bitcast.53), calls=%async_computation.1 | async-start | bytes 1572864 | tf_op jit(solution)/shard_map/all_to_all | solution.py:64
  248.5 70.2 %all-gather.5.cloned.1.call-start = ((), (), s32[]{:S(2)}) async-start(), calls=%async_computation.7 | async-start | bytes 2359296 | tf_op jit(solution)/shard_map/all_gather | solution.py:55
  293.0 182.4 %reduce-scatter.9.cloned.1.call-start = ((), (), s32[]{:S(2)}) async-start(), calls=%async_computation.9 | async-start | bytes 13369344
  494.5 5.5 %copy-start.1 = (f32[128]{0:T(128)S(1)}, f32[128]{0:T(128)}, u32[]{:S(2)}) copy-start(f32[128]{0:T(128)} %param.13) | copy-start | bytes 1540
Sparse Core Ops, SparseCore 0:
  35.7 26.4 all-gather.2
  107.5 134.9 reduce-scatter.6
  293.1 25.5 all-gather.4
  340.5 134.8 reduce-scatter.8
where the time goes:
time: 507 us
  waiting for transfers between devices  325 us (64%)
  blocking collectives  65.1 us (13%)
  matrix products  53.8 us (11%)
  local copies, waits for them, and re-layouts  37.3 us (7%)
  between operations  13.3 us (3%)
  other arithmetic  8.42 us (2%)
    unnamed x6, waiting for transfers between devices  269 us
    all_to_all x2, blocking collectives, body(): lax.all_to_all(rounded, 'cd', split_axis=1, concat_axis=0, tiled=True)  52.4 us
    all_gather x2, waiting for transfers between devices, body(): lax.all_gather(regrouped, 'ab', axis=1, tiled=True)  52 us
    dot_general x2, matrix products, body(): lax.dot_general(lax.all_gather(regrouped, 'ab', axis=1, tiled=True), weig...  44.1 us
    unnamed x11, local copies, waits for them, and re-layouts  16.7 us
    convert_element_type x6, local copies, waits for them, and re-layouts, body(): flip_tiles(tiles, tile_width).astype(jnp.float32)  13.3 us
    all_to_all x1, blocking collectives, body(): lax.all_to_all(swapped.astype(jnp.bfloat16).reshape(rows_dev, ab_count, t...  12.7 us
  transfers between devices with their start and end apart: 5, of which 5 were waited for; matrix products, arithmetic and copies ran while one was open for 1% of the time, Pallas kernels for 0%

commit v1 on v0

--- a/solution.py
+++ b/solution.py
@@ -1,3 +1,4 @@
+import functools
 import jax
 import jax.numpy as jnp
 from jax import lax
@@ -7,6 +8,33 @@
 NOCC = 32
 BLK = 128
 ITERS = 2
+
+
+def state_tasks(sheet, at_axis):
+    sheet = jnp.moveaxis(sheet, 0, at_axis)
+    known = sheet.shape
+    return sheet.reshape(
+        *known[:at_axis], known[at_axis] * known[at_axis + 1], *known[at_axis + 2 :]
+    )
+
+
+def tell_case(incoming_x, ax_name):
+    n_all = lax.axis_size(ax_name)
+    tall = incoming_x[None]
+    for jj in range(n_all.bit_length() - 1):
+        v1 = 1 << jj
+        moved = lax.ppermute(tall, axis_name=ax_name, perm=[(q, q ^ v1) for q in range(n_all)])
+        odd = jnp.stack([tall, moved])
+        all_rows = lax.axis_index(ax_name) >> jj & 1
+        tall = jnp.where(all_rows == 0, odd, odd[::-1]).reshape(-1, *incoming_x.shape)
+    return tall
+
+
+def push_cells(xx, mat, dim_i):
+    return state_tasks(tell_case(xx, mat), dim_i)
+
+
+face_follow = functools.partial(push_cells, mat="ab", dim_i=1)
 
 
 def flip_tiles(tiles, tile_width):
@@ -52,7 +80,7 @@
         rounded = state.astype(jnp.bfloat16)
         regrouped = lax.all_to_all(rounded, "cd", split_axis=1, concat_axis=0, tiled=True)
         partial_value = lax.dot_general(
-            lax.all_gather(regrouped, "ab", axis=1, tiled=True),
+            face_follow(regrouped),
             weights,
             (((1,), (1,)), ((), ())),
             preferred_element_type=jnp.float32,

time: 507 us -> 476 us (0.939)
  waiting for transfers between devices: 325 us -> 308 us
  local copies, waits for them, and re-layouts: 37.3 us -> 22.2 us
    unnamed x6 -> x2, waiting for transfers between devices: 269 us -> 0.03 us
    reduce_scatter x0 -> x2, waiting for transfers between devices: none -> 266 us  [body(): lax.psum_scatter(partial_value.astype(jnp.bfloat16), 'cd', scatter_dimens...]
    all_gather x2 -> x0, waiting for transfers between devices: 52 us -> none  [body(): lax.all_gather(regrouped, 'ab', axis=1, tiled=True)]
    ppermute x0 -> x2, waiting for transfers between devices: none -> 38.8 us  [tell_case(): lax.ppermute(tall, axis_name=ax_name, perm=[(q, q ^ v1) for q in range(n_...]
    unnamed x11 -> x8, local copies, waits for them, and re-layouts: 16.7 us -> 0.02 us
  transfers between devices with their start and end apart: 5 -> 5, of which waited for: 5 -> 5; matrix products, arithmetic and copies ran while one was open for 1% -> 2% of each run, Pallas kernels for 0% -> 0%
where the time goes in v1:
time: 476 us
  waiting for transfers between devices  308 us (65%)
  blocking collectives  64.9 us (14%)
  matrix products  52.5 us (11%)
  local copies, waits for them, and re-layouts  22.2 us (5%)
  between operations  13.6 us (3%)
  other arithmetic  9.27 us (2%)
  starting transfers between devices  5.39 us (1%)
    reduce_scatter x2, waiting for transfers between devices, body(): lax.psum_scatter(partial_value.astype(jnp.bfloat16), 'cd', scatter_dimens...  266 us
    all_to_all x2, blocking collectives, body(): lax.all_to_all(rounded, 'cd', split_axis=1, concat_axis=0, tiled=True)  52.2 us
    dot_general x2, matrix products, body(): lax.dot_general(face_follow(regrouped), weights, (((1,), (1,)), ((), ()))...  42.8 us
    ppermute x2, waiting for transfers between devices, tell_case(): lax.ppermute(tall, axis_name=ax_name, perm=[(q, q ^ v1) for q in range(n_...  38.8 us
    convert_element_type x6, local copies, waits for them, and re-layouts, body(): flip_tiles(tiles, tile_width).astype(jnp.float32)  13.4 us
    all_to_all x1, blocking collectives, body(): lax.all_to_all(swapped.astype(jnp.bfloat16).reshape(rows_dev, ab_count, t...  12.7 us
  transfers between devices with their start and end apart: 5, of which 5 were waited for; matrix products, arithmetic and copies ran while one was open for 2% of the time, Pallas kernels for 0%

profile of v1, /device:TPU:0, one launch (start us, length us, event | category | flops | bytes accessed | tf_op | source)
XLA Modules:
  0.0 476.0 jit_solution(6555994767356325950)
XLA Ops:
  8.1 27.3 %all_to_all.42 = bf16[48,16,512]{2,0,1:T(8,128)(2,1)S(1)} all-to-all(bf16[48,16,512]{2,0,1:T(8,128)(2,1)S(1)} %bitcast.72), channel_id=1, replica_groups=mesh['ab'=2,'cd'=16] {'cd'}, dimensions={1} | all-to-all | bytes 1572864 | tf_op jit(solution)/shard_map/all_to_all | solution.py:81
  35.4 1.5 collective-permute-start
  37.1 18.7 %collective-permute-done = bf16[1,768,512]{2,1,0:T(8,128)(2,1)S(1)} collective-permute-done((bf16[1,768,512]{2,1,0:T(8,128)(2,1)S(1)}, bf16[1,768,512]{2,1,0:T(8,128)(2,1)S(1)}, u32[]{:S(2)}, u32[]{:S(2)}) %collective-permute-start) | collective-permute-done | bytes 786464 | tf_op jit(solution)/shard_map/ppermute | solution.py:26
  57.0 6.1 %mul.31 = bf16[64,128,8,128]{3,2,1,0:T(8,128)(2,1)} broadcast(bf16[64,8]{1,0:T(8,128)(2,1)S(1)} %copy.29), dimensions={0,2} | broadcast | bytes 16778240 | tf_op jit(solution)/shard_map/mul | solution.py:55
  63.1 21.4 %convolution_convert_fusion.1 = bf16[768,8192]{1,0:T(8,128)(2,1)} fusion(bf16[768,1024]{0,1:T(8,128)(2,1)S(1)} %bitcast.82, bf16[8192,1024]{1,0:T(8,128)(2,1)} %param.9, bf16[1024,8,8,128]{3,2,1,0:T(8,128)(2,1)} %bitcast.67), kind=kOutput, calls=%fused_computation.2 | convolution fusion | flops 12899581952 | bytes 47710208 | tf_op jit(solution)/shard_map/dot_general | solution.py:82
  85.3 133.0 %reduce-scatter.3.cloned.1.call-done = bf16[48,8192]{1,0:T(8,128)(2,1)} async-done(((bf16[768,8192]{1,0:T(8,128)(2,1)}), bf16[48,8192]{1,0:T(8,128)(2,1)}) %reduce-scatter.3.cloned.1.call-update) | async-done | bytes 786448 | tf_op jit(solution)/shard_map/reduce_scatter | solution.py:88
  218.3 1.5 convolution_convert_fusion.3
  220.8 3.5 all-to-all-start.1
  224.7 6.4 %fusion = f32[1,8192]{1,0:T(1,128)S(1)} fusion(s32[8192]{0:T(1024)S(1)} %get-tuple-element.9, s32[8192]{0:T(1024)S(1)} %get-tuple-element.8, f32[128]{0:T(128)S(1)} %copy-done), kind=kOutput, calls=%fused_computation.5 | convolution fusion | flops 17825792 | bytes 98816 | tf_op jit(solution)/shard_map/dot_general | solution.py:67
  231.1 3.5 all-to-all-done.1
  234.6 2.4 reshape.159
  237.0 2.4 copy.31
  239.4 1.9 reshape.157
  241.3 2.5 fusion.6
  243.8 24.9 %all_to_all.43 = bf16[48,16,512]{2,0,1:T(8,128)(2,1)S(1)} all-to-all(bf16[48,16,512]{2,0,1:T(8,128)(2,1)S(1)} %bitcast.73), channel_id=1, replica_groups=mesh['ab'=2,'cd'=16] {'cd'}, dimensions={1} | all-to-all | bytes 1572864 | tf_op jit(solution)/shard_map/all_to_all | solution.py:81
  269.0 20.1 %collective-permute-done.1 = bf16[1,768,512]{2,1,0:T(8,128)(2,1)S(1)} collective-permute-done((bf16[1,768,512]{2,1,0:T(8,128)(2,1)S(1)}, bf16[1,768,512]{2,1,0:T(8,128)(2,1)S(1)}, u32[]{:S(2)}, u32[]{:S(2)}) %collective-permute-start.1) | collective-permute-done | bytes 786464 | tf_op jit(solution)/shard_map/ppermute | solution.py:26
  290.2 21.4 %convolution_convert_fusion = bf16[768,8192]{1,0:T(8,128)(2,1)} fusion(bf16[768,1024]{0,1:T(8,128)(2,1)S(1)} %bitcast.83, bf16[8192,1024]{1,0:T(8,128)(2,1)} %param.9, bf16[1024,8,8,128]{3,2,1,0:T(8,128)(2,1)} %bitcast.68), kind=kOutput, calls=%fused_computation.1 | convolution fusion | flops 12899581952 | bytes 47710208 | tf_op jit(solution)/shard_map/dot_general | solution.py:82
  311.6 132.9 %reduce-scatter.5.cloned.1.call-done = bf16[48,8192]{1,0:T(8,128)(2,1)} async-done(((bf16[768,8192]{1,0:T(8,128)(2,1)}), bf16[48,8192]{1,0:T(8,128)(2,1)}) %reduce-scatter.5.cloned.1.call-update) | async-done | bytes 786448 | tf_op jit(solution)/shard_map/reduce_scatter | solution.py:88
  444.5 1.5 convolution_convert_fusion.2
  446.1 12.7 %all_to_all.44 = bf16[48,2,4096]{2,0,1:T(8,128)(2,1)S(1)} all-to-all(bf16[48,2,4096]{2,0,1:T(8,128)(2,1)S(1)} %bitcast.75), channel_id=1, replica_groups=mesh['ab'=2,'cd'=16] {'ab'}, dimensions={1} | all-to-all | bytes 1572864 | tf_op jit(solution)/shard_map/all_to_all | solution.py:92
  458.8 2.4 reshape.160
  461.2 2.4 copy.35
  463.6 1.9 reshape.158
  465.5 3.6 subtract_divide_fusion
  (29 shorter events, 6.5 us)
Async XLA Ops:
  6.5 218.1 %copy-start = (f32[128]{0:T(128)S(1)}, f32[128]{0:T(128)}, u32[]{:S(2)}) copy-start(f32[128]{0:T(128)} %param.13) | copy-start | bytes 1540
  6.5 211.7 %reduce-scatter.3.cloned.1.call-start = ((), (), s32[]{:S(2)}) async-start(), calls=%async_computation.6 | async-start | bytes 13369344 | tf_op jit(solution)/shard_map/reduce_scatter | solution.py:88
  8.0 28.9 %copy-start.2 = (s32[64,8]{0,1:T(8,128)S(1)}, s32[64,8]{0,1:T(8,128)}, u32[]{:S(2)}) copy-start(s32[64,8]{0,1:T(8,128)} %param.10) | copy-start | bytes 6148
  35.4 20.4 %collective-permute-start = (bf16[1,768,512]{2,1,0:T(8,128)(2,1)S(1)}, bf16[1,768,512]{2,1,0:T(8,128)(2,1)S(1)}, u32[]{:S(2)}, u32[]{:S(2)}) collective-permute-start(bf16[1,768,512]{2,1,0:T(8,128)(2,1)S(1)} %bitcast.77), channel_id=1, source_target_pairs={{0,16},{16,0},{1,17},{17,1},{2,18},{18,2},{3,19},{19,3},{4,20},{20... | collective-permute-start | bytes 2359304 | tf_op jit(solution)/shard_map/ppermute | solution.py:26
  219.8 4.6 copy-start.3
  220.8 13.8 %all-to-all-start.1 = ((bf16[48,2,4096]{2,0,1:T(8,128)(2,1)}), bf16[48,2,4096]{2,0,1:T(8,128)(2,1)S(1)}, u32[]{:S(2)}, u32[]{:S(2)}) async-start(bf16[48,2,4096]{2,0,1:T(8,128)(2,1)} %bitcast.65), calls=%async_computation.2 | async-start | bytes 1572864 | tf_op jit(solution)/shard_map/all_to_all | solution.py:92
  224.3 220.2 %reduce-scatter.5.cloned.1.call-start = ((), (), s32[]{:S(2)}) async-start(), calls=%async_computation.7 | async-start | bytes 13369344 | tf_op jit(solution)/shard_map/reduce_scatter | solution.py:88
  268.7 20.4 %collective-permute-start.1 = (bf16[1,768,512]{2,1,0:T(8,128)(2,1)S(1)}, bf16[1,768,512]{2,1,0:T(8,128)(2,1)S(1)}, u32[]{:S(2)}, u32[]{:S(2)}) collective-permute-start(bf16[1,768,512]{2,1,0:T(8,128)(2,1)S(1)} %bitcast.79), channel_id=1, source_target_pairs={{0,16},{16,0},{1,17},{17,1},{2,18},{18,2},{3,19},{19,3},{4,20},{20... | collective-permute-start | bytes 2359304 | tf_op jit(solution)/shard_map/ppermute | solution.py:26
  463.6 5.5 %copy-start.1 = (f32[128]{0:T(128)S(1)}, f32[128]{0:T(128)}, u32[]{:S(2)}) copy-start(f32[128]{0:T(128)} %param.13) | copy-start | bytes 1540
Sparse Core Ops, SparseCore 0:
  84.6 133.6 reduce-scatter.2
  311.8 132.6 reduce-scatter.4
